TPU v7x, 32 devices: a whole 2x2x4 slice. The times are simulated.
32 devices in a mesh: wide: 8 (over z, x), narrow: 4 (over y, core).
Axes of the slice: x: 2, y: 2, z: 4, core: 2. Of those that a mesh axis runs over, the one named last changes fastest.
Arguments:
- points: bfloat16 [32768, 256], P('wide'), may hold values from -6 to 6
- q_init: float32 [16, 32768], P(None, 'wide'), may hold values from -80 to 80
- pairs: int32 [2, 2048], P(None, ('wide', 'narrow')), may hold values from 0 to 255, as said below
Outputs:
- basis: float32 [16, 32768], P(None, 'wide')
- coeffs: float32 [3, 2, 16, 16], replicated
Inputs may be any that keep to these rules, and one draw needn't show every extreme that they name: `pairs`: pair number g * 4 * 64 + m * 64 + o * 8 + c (g < 8, m < 4, o < 8, c < 8) has its first block in g * 32 .. (g + 1) * 32 - 1 and its second block in o * 32 .. (o + 1) * 32 - 1; the two ends of a pair differ.
All inputs are finite; a program needn't handle non-finite values.
Results may differ from a plain program's by a relative error of at most 0.0015.
Values may be sent and summed in bfloat16 or wider, within the bound.
A program may use at most 64 MiB of HBM per device.

v0:
```python
import jax
import jax.numpy as jnp
from jax import lax
from jax.sharding import PartitionSpec as P

BS = 128
STEPS = 3


KERNEL_FACTOR = 3.0
EPSILON = 1e-06
HIGH = lax.Precision.HIGHEST
pair_group = 32


def unit_rows(points):
    wide32 = points.astype(jnp.float32)
    scaled = wide32 * lax.rsqrt(jnp.sum(wide32 * wide32, axis=-1, keepdims=True) + EPSILON)
    return scaled.astype(jnp.bfloat16)


def tile_terms(first_pts, second_pts, first_vec, second_vec):
    inner_products = jnp.einsum(
        "paf,pbf->pab", first_pts, second_pts, preferred_element_type=jnp.float32
    )
    kernel_values = jnp.exp(KERNEL_FACTOR * (inner_products - 1.0))
    to_first = jnp.einsum("pab,prb->pra", kernel_values, second_vec, precision=HIGH)
    to_second = jnp.einsum("pab,pra->prb", kernel_values, first_vec, precision=HIGH)
    return (to_first, to_second)


def per_device(points, q_init, pairs):
    wide_count = lax.axis_size("wide")
    wide_pos = lax.axis_index("wide")
    own_blocks = points.shape[0] // BS
    width = points.shape[1]
    vec_rows = q_init.shape[0]
    pair_count = pairs.shape[1]
    capacity = pair_count // wide_count
    total_points = own_blocks * BS * wide_count
    unit = unit_rows(points).reshape(own_blocks, BS, width)
    first_local = pairs[0] - wide_pos * own_blocks
    wanted = pairs[1].reshape(wide_count, capacity)
    local_ids = (
        lax.all_to_all(wanted, "wide", split_axis=0, concat_axis=0, tiled=True)
        - wide_pos * own_blocks
    )
    replies = lax.all_to_all(unit[local_ids], "wide", split_axis=0, concat_axis=0, tiled=True)
    second_pts = replies
    second_pts = second_pts.reshape(pair_count, BS, width)
    targets = jnp.concatenate([first_local, local_ids.reshape(pair_count)], axis=0)
    owners = (jnp.arange(own_blocks, dtype=jnp.int32)[:, None] == targets[None, :]).astype(
        jnp.float32
    )

    def grouped(values):
        return values.reshape((pair_count // pair_group, pair_group) + values.shape[1:])

    def single_group(items):
        first_ids, second_p, first_v, second_v = items
        return tile_terms(unit[first_ids], second_p, first_v, second_v)

    def gram_sums(values):
        return lax.psum(values, "wide")

    gram0 = gram_sums(jnp.dot(q_init, q_init.T, precision=HIGH)) / total_points
    factor0 = jnp.linalg.cholesky(gram0)
    present_portion = lax.linalg.triangular_solve(factor0, q_init, left_side=True, lower=True)
    current = present_portion
    previous = jnp.zeros_like(present_portion)
    last = jnp.zeros((vec_rows, vec_rows), jnp.float32)
    records = []
    for step in range(STEPS):
        rows = current.reshape(vec_rows, own_blocks, BS).transpose(1, 0, 2)
        second_vec = lax.all_to_all(
            rows[local_ids], "wide", split_axis=0, concat_axis=0, tiled=True
        ).reshape(pair_count, vec_rows, BS)
        first_vec = rows[first_local]
        to_first, to_second = lax.map(
            single_group,
            (grouped(first_local), grouped(second_pts), grouped(first_vec), grouped(second_vec)),
        )
        to_first = to_first.reshape(pair_count, vec_rows * BS)
        returned = lax.all_to_all(
            to_second.reshape(wide_count, capacity, vec_rows * BS),
            "wide",
            split_axis=0,
            concat_axis=0,
            tiled=True,
        )
        terms = jnp.concatenate([to_first, returned.reshape(pair_count, vec_rows * BS)], axis=0)
        summed_blocks = jnp.dot(owners, terms, precision=HIGH)
        summed_blocks = lax.psum(summed_blocks, "narrow")
        image = summed_blocks.reshape(-1, vec_rows, BS).transpose(1, 0, 2).reshape(vec_rows, -1)
        residual = image - jnp.dot(last.T, previous, precision=HIGH)
        raw, cross, basis_gram = gram_sums(
            (
                jnp.dot(residual, residual.T, precision=HIGH),
                jnp.dot(present_portion, residual.T, precision=HIGH),
                jnp.dot(present_portion, present_portion.T, precision=HIGH),
            )
        )
        along = cross / total_points
        raw = raw / total_points
        basis_gram = basis_gram / total_points
        remainder = residual - jnp.dot(along.T, present_portion, precision=HIGH)
        squared = jnp.dot(along.T, along, precision=HIGH)
        gram = (
            raw
            - 2.0 * squared
            + jnp.dot(along.T, jnp.dot(basis_gram, along, precision=HIGH), precision=HIGH)
        )
        factor = jnp.linalg.cholesky(gram)
        records.append(jnp.stack([along, factor]))
        previous = present_portion
        last = factor
        present_portion = lax.linalg.triangular_solve(factor, remainder, left_side=True, lower=True)
        current = present_portion
    return (current, jnp.stack(records))


def solution(mesh):
    placed = (P("wide", None), P(None, "wide"), P(None, ("wide", "narrow")))
    return jax.shard_map(
        per_device, mesh=mesh, in_specs=placed, out_specs=(P(None, "wide"), P()), check_vma=False
    )
```

profile of v0, /device:TPU:0, one launch (start us, length us, event | category | flops | bytes accessed | tf_op | source)
XLA Modules:
  0.0 559.8 jit_solution(13503507722654973966)
XLA Ops:
  8.6 7.3 %all-to-all-start = ((s32[8,1,8]{2,1,0:T(1,128)}), s32[8,1,8]{2,1,0:T(1,128)S(1)}, u32[]{:S(2)}, u32[]{:S(2)}) async-start(s32[8,1,8]{2,1,0:T(1,128)} %bitcast.22), calls=%async_computation | async-start | bytes 8192 | tf_op jit(solution)/shard_map/all_to_all | solution.py:45
  16.4 22.1 %psum.91 = f32[16,16]{1,0:T(8,128)S(1)} all-reduce(f32[16,16]{1,0:T(8,128)S(1)} %fusion.187), channel_id=1, replica_groups=mesh['wide'=8,'narrow'=4] {'wide'}, use_global_device_ids=true, to_apply=%region_1.0 | all-reduce | flops 256 | bytes 2048 | tf_op jit(solution)/shard_map/psum | solution.py:64
  43.1 2.2 fusion.78
  46.9 3.5 all-to-all-start.1
  52.3 2.8 gather_fusion.4
  55.1 5.6 %all-to-all-done.1 = f32[8,8,16,128]{3,2,1,0:T(8,128)S(1)} async-done(((f32[8,8,16,128]{3,2,1,0:T(8,128)}), f32[8,8,16,128]{3,2,1,0:T(8,128)S(1)}, u32[]{:S(2)}, u32[]{:S(2)}) %all-to-all-start.1) | async-done | bytes 524320 | tf_op jit(solution)/shard_map/all_to_all | solution.py:75
  60.7 4.7 all-to-all-start.2
  67.0 87.2 %all-to-all-done.2 = bf16[8,8,128,256]{3,2,1,0:T(8,128)(2,1)} async-done(((bf16[8,8,128,256]{3,2,1,0:T(8,128)(2,1)}), bf16[8,8,128,256]{3,2,1,0:T(8,128)(2,1)}, u32[]{:S(2)}, u32[]{:S(2)}) %all-to-all-start.2) | async-done | bytes 4194336 | tf_op jit(solution)/shard_map/all_to_all | solution.py:48
  155.9 23.6 %while.42 = (s32[]{:T(128)}, f32[2,32,16,128]{3,2,1,0:T(8,128)}, f32[2,32,16,128]{3,2,1,0:T(8,128)}, f32[2,32,16,128]{3,2,1,0:T(8,128)S(1)}, s32[2,32]{1,0:T(2,1...) while((s32[]{:T(128)}, f32[2,32,16,128]{3,2,1,0:T(8,128)}, ...), condition=%wide.region_5.8_spmd, body=%wide.region_4.7_spmd.sunk | while | flops 471860320 | bytes 17833084 | solution.py:79
  155.9 2.0 gather_fusion
  158.0 2.9 fusion.264
  160.9 4.1 fusion.265
  165.0 2.8 fusion.266
  169.8 2.9 fusion.264
  172.7 4.1 fusion.265
  176.8 2.8 fusion.266
  181.5 3.5 all-to-all-start.3
  185.2 2.0 copy.75
  187.2 12.4 %all-to-all-done.3 = f32[8,8,2048]{2,1,0:T(8,128)S(1)} async-done(((f32[8,8,2048]{2,1,0:T(8,128)}), f32[8,8,2048]{2,1,0:T(8,128)S(1)}, u32[]{:S(2)}, u32[]{:S(2)}) %all-to-all-start.3) | async-done | bytes 524320 | tf_op jit(solution)/shard_map/all_to_all | solution.py:84
  202.4 31.1 %all-reduce.7.cloned.1.call-done = f32[16,4096]{1,0:T(8,128)} async-done(((f32[16,4096]{1,0:T(8,128)}), f32[16,4096]{1,0:T(8,128)}) %all-reduce.7.cloned.1.call-update) | async-done | bytes 262160 | tf_op jit(solution)/shard_map/psum | solution.py:93
  235.6 37.1 %all-reduce.2 = (f32[16,16]{1,0:T(8,128)S(1)}, f32[16,16]{1,0:T(8,128)S(1)}, f32[16,16]{1,0:T(8,128)S(1)}) all-reduce(f32[16,16]{1,0:T(8,128)S(1)} %fusion.189, f32[16,16]{1,0:T(8,128)S(1)} %fusion.188, f32[16,16]{1,0:T(8,128)S(1)} %fusion.190), channel_id=1, replica_groups=mesh['wide'=8,'narrow'=4] {'wide'}, use_global_device_ids=true, to_apply=%region_8.11 | all-reduce | flops 768 | bytes 6144 | tf_op jit(solution)/shard_map/psum | solution.py:64
  279.7 4.1 all-to-all-start.4
  285.3 8.8 %all-to-all-done.4 = f32[8,8,16,128]{3,2,1,0:T(8,128)} async-done(((f32[8,8,16,128]{3,2,1,0:T(8,128)}), f32[8,8,16,128]{3,2,1,0:T(8,128)}, u32[]{:S(2)}, u32[]{:S(2)}) %all-to-all-start.4) | async-done | bytes 524320 | tf_op jit(solution)/shard_map/all_to_all | solution.py:75
  295.8 25.6 %while.43 = (s32[]{:T(128)}, f32[2,32,16,128]{3,2,1,0:T(8,128)}, f32[2,32,16,128]{3,2,1,0:T(8,128)}, f32[2,32,16,128]{3,2,1,0:T(8,128)}, s32[2,32]{1,0:T(2,128)S...) while((s32[]{:T(128)}, f32[2,32,16,128]{3,2,1,0:T(8,128)}, ...), condition=%wide.region_11.14_spmd, body=%wide.region_10.13_spmd.sunk | while | flops 471860320 | bytes 17833084 | solution.py:79
  297.8 2.9 fusion.272
  300.7 5.1 fusion.273
  305.8 2.7 fusion.274
  310.6 2.9 fusion.272
  313.5 5.1 fusion.273
  318.6 2.8 fusion.274
  323.2 3.7 all-to-all-start.5
  326.9 2.0 copy.74
  329.0 8.2 %all-to-all-done.5 = f32[8,8,2048]{2,1,0:T(8,128)S(1)} async-done(((f32[8,8,2048]{2,1,0:T(8,128)}), f32[8,8,2048]{2,1,0:T(8,128)S(1)}, u32[]{:S(2)}, u32[]{:S(2)}) %all-to-all-start.5) | async-done | bytes 524320 | tf_op jit(solution)/shard_map/all_to_all | solution.py:84
  339.9 30.2 %all-reduce.9.cloned.1.call-done = f32[16,4096]{1,0:T(8,128)} async-done(((f32[16,4096]{1,0:T(8,128)}), f32[16,4096]{1,0:T(8,128)}) %all-reduce.9.cloned.1.call-update) | async-done | bytes 262160 | tf_op jit(solution)/shard_map/psum | solution.py:93
  373.0 37.1 %all-reduce.1 = (f32[16,16]{1,0:T(8,128)S(1)}, f32[16,16]{1,0:T(8,128)S(1)}, f32[16,16]{1,0:T(8,128)S(1)}) all-reduce(f32[16,16]{1,0:T(8,128)S(1)} %fusion.192, f32[16,16]{1,0:T(8,128)S(1)} %fusion.191, f32[16,16]{1,0:T(8,128)S(1)} %fusion.193), channel_id=1, replica_groups=mesh['wide'=8,'narrow'=4] {'wide'}, use_global_device_ids=true, to_apply=%region_14.17 | all-reduce | flops 768 | bytes 6144 | tf_op jit(solution)/shard_map/psum | solution.py:64
  417.0 4.4 all-to-all-start.6
  422.8 8.6 %all-to-all-done.6 = f32[8,8,16,128]{3,2,1,0:T(8,128)} async-done(((f32[8,8,16,128]{3,2,1,0:T(8,128)}), f32[8,8,16,128]{3,2,1,0:T(8,128)}, u32[]{:S(2)}, u32[]{:S(2)}) %all-to-all-start.6) | async-done | bytes 524320 | tf_op jit(solution)/shard_map/all_to_all | solution.py:75
  433.1 25.6 %while.44 = (s32[]{:T(128)}, f32[2,32,16,128]{3,2,1,0:T(8,128)}, f32[2,32,16,128]{3,2,1,0:T(8,128)}, f32[2,32,16,128]{3,2,1,0:T(8,128)}, s32[2,32]{1,0:T(2,128)S...) while((s32[]{:T(128)}, f32[2,32,16,128]{3,2,1,0:T(8,128)}, ...), condition=%wide.region_17.20_spmd, body=%wide.region_16.19_spmd.sunk | while | flops 471860320 | bytes 17833084 | solution.py:79
  435.1 2.9 fusion.280
  438.0 5.1 fusion.281
  443.1 2.7 fusion.282
  447.9 2.9 fusion.280
  450.8 5.1 fusion.281
  455.9 2.8 fusion.282
  460.6 3.7 all-to-all-start.7
  466.0 8.5 %all-to-all-done.7 = f32[8,8,2048]{2,1,0:T(8,128)S(1)} async-done(((f32[8,8,2048]{2,1,0:T(8,128)}), f32[8,8,2048]{2,1,0:T(8,128)S(1)}, u32[]{:S(2)}, u32[]{:S(2)}) %all-to-all-start.7) | async-done | bytes 524320 | tf_op jit(solution)/shard_map/all_to_all | solution.py:84
  475.8 30.6 %all-reduce.11.cloned.1.call-done = f32[16,4096]{1,0:T(8,128)} async-done(((f32[16,4096]{1,0:T(8,128)}), f32[16,4096]{1,0:T(8,128)}) %all-reduce.11.cloned.1.call-update) | async-done | bytes 262160 | tf_op jit(solution)/shard_map/psum | solution.py:93
  509.3 37.1 %all-reduce = (f32[16,16]{1,0:T(8,128)S(1)}, f32[16,16]{1,0:T(8,128)S(1)}, f32[16,16]{1,0:T(8,128)S(1)}) all-reduce(f32[16,16]{1,0:T(8,128)S(1)} %fusion.195, f32[16,16]{1,0:T(8,128)S(1)} %fusion.194, f32[16,16]{1,0:T(8,128)S(1)} %fusion.196), channel_id=1, replica_groups=mesh['wide'=8,'narrow'=4] {'wide'}, use_global_device_ids=true, to_apply=%region_20.23 | all-reduce | flops 768 | bytes 6144 | tf_op jit(solution)/shard_map/psum | solution.py:64
  (147 shorter events, 72.6 us)
Async XLA Ops:
  7.2 8.8 %copy-start = (f32[16,4096]{1,0:T(8,128)S(1)}, f32[16,4096]{1,0:T(8,128)}, u32[]{:S(2)}) copy-start(f32[16,4096]{1,0:T(8,128)} %param.13) | copy-start | bytes 786436
  8.6 36.7 %all-to-all-start = ((s32[8,1,8]{2,1,0:T(1,128)}), s32[8,1,8]{2,1,0:T(1,128)S(1)}, u32[]{:S(2)}, u32[]{:S(2)}) async-start(s32[8,1,8]{2,1,0:T(1,128)} %bitcast.22), calls=%async_computation | async-start | bytes 8192 | tf_op jit(solution)/shard_map/all_to_all | solution.py:45
  46.9 13.9 %all-to-all-start.1 = ((f32[8,8,16,128]{3,2,1,0:T(8,128)}), f32[8,8,16,128]{3,2,1,0:T(8,128)S(1)}, u32[]{:S(2)}, u32[]{:S(2)}) async-start(f32[8,8,16,128]{3,2,1,0:T(8,128)} %bitcast.29), calls=%async_computation.1 | async-start | bytes 1048576 | tf_op jit(solution)/shard_map/all_to_all | solution.py:75
  60.7 4.7 copy-start.4
  60.7 93.5 %all-to-all-start.2 = ((bf16[8,8,128,256]{3,2,1,0:T(8,128)(2,1)}), bf16[8,8,128,256]{3,2,1,0:T(8,128)(2,1)}, u32[]{:S(2)}, u32[]{:S(2)}) async-start(bf16[8,8,128,256]{3,2,1,0:T(8,128)(2,1)} %bitcast.312), calls=%async_computation.2 | async-start | bytes 8388608 | tf_op jit(solution)/shard_map/all_to_all | solution.py:48
  160.9 4.1 copy-start.2
  172.7 4.1 copy-start.2
  181.5 18.2 %all-to-all-start.3 = ((f32[8,8,2048]{2,1,0:T(8,128)}), f32[8,8,2048]{2,1,0:T(8,128)S(1)}, u32[]{:S(2)}, u32[]{:S(2)}) async-start(f32[8,8,2048]{2,1,0:T(8,128)} %reshape.254), calls=%async_computation.3 | async-start | bytes 1048576 | tf_op jit(solution)/shard_map/all_to_all | solution.py:84
  185.0 48.6 %all-reduce.7.cloned.1.call-start = ((), (), s32[]{:S(2)}) async-start(), calls=%async_computation.8 | async-start | bytes 524288 | tf_op jit(solution)/shard_map/psum | solution.py:93
  279.7 14.4 %all-to-all-start.4 = ((f32[8,8,16,128]{3,2,1,0:T(8,128)}), f32[8,8,16,128]{3,2,1,0:T(8,128)}, u32[]{:S(2)}, u32[]{:S(2)}) async-start(f32[8,8,16,128]{3,2,1,0:T(8,128)} %bitcast.324), calls=%async_computation.4 | async-start | bytes 1048576 | tf_op jit(solution)/shard_map/all_to_all | solution.py:75
  300.7 5.1 copy-start.3
  313.5 5.1 copy-start.3
  323.2 13.9 %all-to-all-start.5 = ((f32[8,8,2048]{2,1,0:T(8,128)}), f32[8,8,2048]{2,1,0:T(8,128)S(1)}, u32[]{:S(2)}, u32[]{:S(2)}) async-start(f32[8,8,2048]{2,1,0:T(8,128)} %reshape.261), calls=%async_computation.5 | async-start | bytes 1048576 | tf_op jit(solution)/shard_map/all_to_all | solution.py:84
  326.9 43.2 %all-reduce.9.cloned.1.call-start = ((), (), s32[]{:S(2)}) async-start(), calls=%async_computation.9 | async-start | bytes 524288 | tf_op jit(solution)/shard_map/psum | solution.py:93
  417.0 14.4 %all-to-all-start.6 = ((f32[8,8,16,128]{3,2,1,0:T(8,128)}), f32[8,8,16,128]{3,2,1,0:T(8,128)}, u32[]{:S(2)}, u32[]{:S(2)}) async-start(f32[8,8,16,128]{3,2,1,0:T(8,128)} %bitcast.323), calls=%async_computation.6 | async-start | bytes 1048576 | tf_op jit(solution)/shard_map/all_to_all | solution.py:75
  438.0 5.1 copy-start.1
  450.8 5.1 copy-start.1
  460.6 13.9 %all-to-all-start.7 = ((f32[8,8,2048]{2,1,0:T(8,128)}), f32[8,8,2048]{2,1,0:T(8,128)S(1)}, u32[]{:S(2)}, u32[]{:S(2)}) async-start(f32[8,8,2048]{2,1,0:T(8,128)} %reshape.268), calls=%async_computation.7 | async-start | bytes 1048576 | tf_op jit(solution)/shard_map/all_to_all | solution.py:84
  464.2 42.2 %all-reduce.11.cloned.1.call-start = ((), (), s32[]{:S(2)}) async-start(), calls=%async_computation.10 | async-start | bytes 524288 | tf_op jit(solution)/shard_map/psum | solution.py:93
Sparse Core Ops, SparseCore 0:
  202.1 31.3 all-reduce.6
  339.6 30.4 all-reduce.8
  475.9 30.4 all-reduce.10
where the time goes:
time: 561 us; the launch traced here: 560 us
  waiting for transfers between devices  231 us (41%)
  blocking collectives  133 us (24%)
  matrix products  80.9 us (14%)
  local copies, waits for them, and re-layouts  43.4 us (8%)
  starting transfers between devices  34.9 us (6%)
  other arithmetic  21.7 us (4%)
  between operations  14.1 us (3%)
    psum x4, blocking collectives, gram_sums(): return lax.psum(values, 'wide')  133 us
    psum x3, waiting for transfers between devices, per_device(): summed_blocks = lax.psum(summed_blocks, 'narrow')  91.8 us
    all_to_all x1, waiting for transfers between devices, per_device(): lax.all_to_all(unit[local_ids], 'wide', split_axis=0, concat_axis=0, tile...  87.2 us
    all_to_all x3, waiting for transfers between devices, per_device(): lax.all_to_all(to_second.reshape(wide_count, capacity, vec_rows * BS), 'w...  29.2 us
    dot_general x6, matrix products, tile_terms(): jnp.einsum('pab,prb->pra', kernel_values, second_vec, precision=HIGH)  28.5 us
    all_to_all x3, waiting for transfers between devices, per_device(): lax.all_to_all(rows[local_ids], 'wide', split_axis=0, concat_axis=0, tile...  23.1 us
    dot_general x6, matrix products, tile_terms(): jnp.einsum('paf,pbf->pab', first_pts, second_pts, preferred_element_type=...  17.6 us
    dot_general x6, matrix products, tile_terms(): jnp.einsum('pab,pra->prb', kernel_values, first_vec, precision=HIGH)  16.5 us
  transfers between devices with their start and end apart: 11, of which 10 were waited for; matrix products, arithmetic and copies ran while one was open for 4% of the time, Pallas kernels for 0%

commit v1 on v0

v1 whole, which is shorter than its diff:
```python
import functools

import jax
import jax.numpy as jnp
from jax import lax
from jax.experimental import pallas as pl
from jax.experimental.pallas import tpu as pltpu
from jax.sharding import PartitionSpec as P

BS = 128
STEPS = 3
KERNEL_FACTOR = 3.0
EPSILON = 1e-06
HIGH = lax.Precision.HIGHEST
MESH = pl.DeviceIdType.MESH


def unit_rows(points):
    wide32 = points.astype(jnp.float32)
    scaled = wide32 * lax.rsqrt(jnp.sum(wide32 * wide32, axis=-1, keepdims=True) + EPSILON)
    return scaled.astype(jnp.bfloat16)


def split(x):
    high = x.astype(jnp.bfloat16)
    return high, (x - high.astype(jnp.float32)).astype(jnp.bfloat16)


def dot32(a, b):
    return jnp.dot(a, b, precision=HIGH, preferred_element_type=jnp.float32)


def dot_nt(a, b, precision=None):
    return lax.dot_general(
        a, b, (((1,), (1,)), ((), ())), precision=precision, preferred_element_type=jnp.float32
    )


def tiles_kernel(capacity, me_ref, first_ref, unit_ref, second_ref, out_ref):
    d = pl.program_id(0)
    for c in range(capacity):
        s = dot_nt(unit_ref[first_ref[d * capacity + c]], second_ref[0, c])
        high, low = split(jnp.exp(KERNEL_FACTOR * (s - 1.0)))
        out_ref[c, :, :BS] = high
        out_ref[c, :, BS:] = low


def make_tiles(me, first, unit, second):
    wide_count, capacity, _, width = second.shape
    own_blocks = unit.shape[0]
    spec = pltpu.PrefetchScalarGridSpec(
        num_scalar_prefetch=2,
        grid=(wide_count,),
        in_specs=[
            pl.BlockSpec((own_blocks, BS, width), lambda d, m, f: (0, 0, 0)),
            pl.BlockSpec(
                (1, capacity, BS, width),
                lambda d, m, f: (lax.rem(m[0] - d + wide_count, wide_count), 0, 0, 0),
            ),
        ],
        out_specs=pl.BlockSpec((capacity, BS, 2 * BS), lambda d, m, f: (d, 0, 0)),
    )
    return pl.pallas_call(
        functools.partial(tiles_kernel, capacity),
        grid_spec=spec,
        out_shape=jax.ShapeDtypeStruct((wide_count * capacity, BS, 2 * BS), jnp.bfloat16),
        name="tiles",
    )(me, first, unit, second)


def factor_of(gram, r):
    i = lax.broadcasted_iota(jnp.int32, (r, r), 0)
    j = lax.broadcasted_iota(jnp.int32, (r, r), 1)
    both_i = lax.broadcasted_iota(jnp.int32, (r, 2 * r), 0)
    m = jnp.concatenate([gram, (i == j).astype(jnp.float32)], axis=1)
    lower = jnp.zeros((r, r), jnp.float32)
    for k in range(r):
        inv = 1.0 / jnp.sqrt(m[k : k + 1, k : k + 1])
        row = m[k : k + 1, :] * inv
        col = m[:, k : k + 1] * inv
        lower = jnp.where((j == k) & (i >= k), col, lower)
        m = jnp.where(both_i == k, row, jnp.where(both_i > k, m - col * row, m))
    upper = jnp.where(j >= i, m[:, :r], 0.0)
    inverse = jnp.where(j <= i, m[:, r:], 0.0)
    return lower, upper, inverse


def main_kernel(
    dims, first, local, owners, tiles, q_ref, out, coef,
    sb, rb, sb2, rb2, tf, pb, rs, ag, xs, blocks, prev, up, gs, gr,
    s1, r1, s2, r2, s3, r3, s4, r4, s5, r5,
):
    W, N, C, R, B, total = dims
    CR = C * R
    RN = R // N
    PR = RN * B
    me = lax.axis_index("wide")
    nar = lax.axis_index("narrow")

    def up_peer(d):
        return lax.rem(me + d, W)

    def down_peer(d):
        return lax.rem(me - d + W, W)

    barrier = pltpu.get_barrier_semaphore()
    for d in range(1, W):
        pl.semaphore_signal(barrier, inc=1, device_id={"wide": up_peer(d)}, device_id_type=MESH)
    for d in range(1, N):
        pl.semaphore_signal(
            barrier, inc=1, device_id={"narrow": lax.rem(nar + d, N)}, device_id_type=MESH
        )
    pl.semaphore_wait(barrier, W - 1 + N - 1)

    def request(d):
        rows = pl.ds(d * CR, CR)
        return pltpu.make_async_remote_copy(
            src_ref=sb.at[rows], dst_ref=rb.at[rows], send_sem=s1.at[d], recv_sem=r1.at[d],
            device_id={"wide": up_peer(d)}, device_id_type=MESH,
        )

    def answer(d):
        rows = pl.ds(d * CR, CR)
        return pltpu.make_async_remote_copy(
            src_ref=sb2.at[rows], dst_ref=rb2.at[rows], send_sem=s2.at[d], recv_sem=r2.at[d],
            device_id={"wide": down_peer(d)}, device_id_type=MESH,
        )

    def scatter(d):
        return pltpu.make_async_remote_copy(
            src_ref=pb.at[pl.ds(lax.rem(nar + d, N) * PR, PR)], dst_ref=rs.at[d],
            send_sem=s3.at[d], recv_sem=r3.at[d],
            device_id={"narrow": lax.rem(nar + d, N)}, device_id_type=MESH,
        )

    def gather(d):
        mine = pl.ds(nar * PR, PR)
        return pltpu.make_async_remote_copy(
            src_ref=rs.at[0], dst_ref=ag.at[mine], send_sem=s4.at[d], recv_sem=r4.at[d],
            device_id={"narrow": lax.rem(nar + d, N)}, device_id_type=MESH,
        )

    def gathered(d):
        theirs = pl.ds(lax.rem(nar - d + N, N) * PR, PR)
        return pltpu.make_async_remote_copy(
            src_ref=rs.at[0], dst_ref=ag.at[theirs], send_sem=s4.at[d], recv_sem=r4.at[d],
            device_id={"narrow": lax.rem(nar + d, N)}, device_id_type=MESH,
        )

    def gram_copy(d):
        return pltpu.make_async_remote_copy(
            src_ref=gs, dst_ref=gr.at[d], send_sem=s5.at[d], recv_sem=r5.at[d],
            device_id={"wide": up_peer(d)}, device_id_type=MESH,
        )

    def gram_sum(value):
        gs[:, : 2 * R] = value
        gr[0, :, : 2 * R] = value
        for d in range(1, W):
            gram_copy(d).start()
        for d in range(1, W):
            gram_copy(d).wait_recv()
        summed = jnp.zeros((2 * R, 2 * R), jnp.float32)
        for s in range(W):
            summed += gr[lax.rem(me - s + W, W)][:, : 2 * R]
        for d in range(1, W):
            gram_copy(d).wait_send()
        return summed / total

    gs[...] = jnp.zeros_like(gs)
    xs[:R, :] = q_ref[...]
    xs[R:, :] = jnp.zeros((R, B * BS), jnp.float32)
    prev[...] = jnp.zeros_like(prev)
    up[...] = jnp.zeros_like(up)
    start = gram_sum(dot_nt(xs[...], xs[...], HIGH))
    _, _, inverse0 = factor_of(start[:R, :R], R)
    xs[:R, :] = dot32(inverse0, q_ref[...])

    def step(k, carry):
        for b in range(B):
            blocks[b] = xs[:R, b * BS : (b + 1) * BS]
        for d in range(W):
            for c in range(C):
                value = blocks[local[d * C + c]]
                (rb if d == 0 else sb)[pl.ds((d * C + c) * R, R), :] = value
            if d:
                request(d).start()

        def group(d, carry):
            @pl.when(d > 0)
            def _():
                request(d).wait_recv()

            for c in range(C):
                p = d * C + c
                rows = pl.ds(pl.multiple_of(p * R, R), R)
                tile = tiles[p]
                high, low = split(rb[rows, :])
                left = jnp.concatenate(
                    [
                        jnp.concatenate([high, high], axis=1),
                        jnp.concatenate([low, jnp.zeros_like(low)], axis=1),
                    ],
                    axis=0,
                )
                both = dot_nt(left, tile)
                tf[rows, :] = both[:R] + both[R:]
                high, low = split(blocks[first[p]])
                both = jnp.dot(
                    jnp.concatenate([high, low], axis=0), tile, preferred_element_type=jnp.float32
                )
                sb2[rows, :] = both[:R, :BS] + both[R:, :BS] + both[:R, BS:]

            @pl.when(d > 0)
            def _():
                answer(d).start()

            return carry

        lax.fori_loop(0, W, group, 0)
        rb2[pl.ds(0, CR), :] = sb2[pl.ds(0, CR), :]
        for d in range(1, W):
            answer(d).wait_recv()

        one_hot = owners[...]
        for n in range(1, N + 1):
            part = lax.rem(nar + n, N)
            for q in range(RN):
                r = part * RN + q
                x = jnp.concatenate(
                    [tf[pl.ds(r, W * C, stride=R), :], rb2[pl.ds(r, W * C, stride=R), :]], axis=0
                )
                high, low = split(x)
                value = jnp.dot(
                    one_hot,
                    jnp.concatenate([high, low], axis=0),
                    preferred_element_type=jnp.float32,
                )
                if n == N:
                    rs[0, pl.ds(q * B, B), :] = value
                else:
                    pb[pl.ds(pl.multiple_of(part * PR + q * B, B), B), :] = value
            if n < N:
                scatter(n).start()
        for d in range(1, N):
            scatter(d).wait_recv()
        mine = rs[0]
        for d in range(1, N):
            mine += rs[d]
        rs[0] = mine
        for d in range(1, N):
            gather(d).start()
        ag[pl.ds(pl.multiple_of(nar * PR, PR), PR), :] = mine
        for d in range(1, N):
            gathered(d).wait_recv()

        for b in range(B):
            xs[R:, b * BS : (b + 1) * BS] = ag[pl.ds(b, R, stride=B), :]
        xs[R:, :] = xs[R:, :] - dot32(up[...], prev[...])
        summed = gram_sum(dot_nt(xs[...], xs[...], HIGH))
        basis_gram = summed[:R, :R]
        along = summed[:R, R:]
        along_t = summed[R:, :R]
        raw = summed[R:, R:]
        gram = raw - 2.0 * dot32(along_t, along) + dot32(along_t, dot32(basis_gram, along))
        lower, upper, inverse = factor_of(gram, R)
        coef[k, 0] = along
        coef[k, 1] = lower
        prev[...] = xs[:R, :]
        up[...] = upper
        mix = jnp.concatenate([-dot32(inverse, along_t), inverse], axis=1)
        xs[:R, :] = dot32(mix, xs[...])

        for d in range(1, W):
            request(d).wait_send()
            answer(d).wait_send()
        for d in range(1, N):
            scatter(d).wait_send()
            gather(d).wait_send()
        return carry

    lax.fori_loop(0, STEPS, step, 0)
    out[...] = xs[:R, :]


def lanczos(first, local, owners, tiles, q_init, wide_count, narrow_count, total):
    R, cols = q_init.shape
    B = cols // BS
    pair_count = first.shape[0]
    C = pair_count // wide_count
    dims = (wide_count, narrow_count, C, R, B, total)
    vmem = pl.BlockSpec(memory_space=pltpu.VMEM)
    smem = pl.BlockSpec(memory_space=pltpu.SMEM)
    f32 = jnp.float32
    pairs_buf = pltpu.VMEM((pair_count * R, BS), f32)
    part = R // narrow_count * B
    wide_sem = pltpu.SemaphoreType.DMA((wide_count,))
    narrow_sem = pltpu.SemaphoreType.DMA((narrow_count,))
    return pl.pallas_call(
        functools.partial(main_kernel, dims),
        out_shape=(
            jax.ShapeDtypeStruct((R, cols), f32),
            jax.ShapeDtypeStruct((STEPS, 2, R, R), f32),
        ),
        in_specs=[smem, smem, vmem, vmem, vmem],
        out_specs=(vmem, vmem),
        scratch_shapes=[
            pairs_buf, pairs_buf, pairs_buf, pairs_buf, pairs_buf,
            pltpu.VMEM((R * B, BS), f32),
            pltpu.VMEM((narrow_count, part, BS), f32),
            pltpu.VMEM((R * B, BS), f32),
            pltpu.VMEM((2 * R, cols), f32),
            pltpu.VMEM((B, R, BS), f32),
            pltpu.VMEM((R, cols), f32),
            pltpu.VMEM((R, R), f32),
            pltpu.VMEM((2 * R, BS), f32),
            pltpu.VMEM((wide_count, 2 * R, BS), f32),
            wide_sem, wide_sem, wide_sem, wide_sem,
            narrow_sem, narrow_sem, narrow_sem, narrow_sem,
            wide_sem, wide_sem,
        ],
        compiler_params=pltpu.CompilerParams(collective_id=0, has_side_effects=True),
        name="lanczos",
    )(first, local, owners, tiles, q_init)


def per_device(points, q_init, pairs):
    wide_count = lax.axis_size("wide")
    narrow_count = lax.axis_size("narrow")
    me = lax.axis_index("wide")
    own_blocks = points.shape[0] // BS
    width = points.shape[1]
    pair_count = pairs.shape[1]
    capacity = pair_count // wide_count
    total = own_blocks * BS * wide_count
    unit = unit_rows(points).reshape(own_blocks, BS, width)
    wanted = pairs[1].reshape(wide_count, capacity)
    local_ids = (
        lax.all_to_all(wanted, "wide", split_axis=0, concat_axis=0, tiled=True) - me * own_blocks
    )
    second = lax.all_to_all(unit[local_ids], "wide", split_axis=0, concat_axis=0, tiled=True)
    turn = jnp.arange(wide_count, dtype=jnp.int32)
    first_rows = (pairs[0] - me * own_blocks).reshape(wide_count, capacity)
    first = first_rows[(me - turn) % wide_count].reshape(pair_count)
    local = local_ids.reshape(wide_count, capacity)[(me + turn) % wide_count].reshape(pair_count)
    targets = jnp.concatenate([first, local, first, local])
    owners = (jnp.arange(own_blocks, dtype=jnp.int32)[:, None] == targets[None, :]).astype(
        jnp.bfloat16
    )
    tiles = make_tiles(jnp.reshape(me, (1,)).astype(jnp.int32), first, unit, second.reshape(wide_count, capacity, BS, width))
    return lanczos(first, local, owners, tiles, q_init, wide_count, narrow_count, total)


def solution(mesh):
    placed = (P("wide", None), P(None, "wide"), P(None, ("wide", "narrow")))
    return jax.shard_map(
        per_device, mesh=mesh, in_specs=placed, out_specs=(P(None, "wide"), P()), check_vma=False
    )
```

time: 561 us -> 273 us (0.49)
  Pallas kernels: 0 us -> 153 us
  waiting for transfers between devices: 231 us -> 92.1 us
  blocking collectives: 133 us -> 0 us
  matrix products: 80.9 us -> 0 us
  local copies, waits for them, and re-layouts: 43.4 us -> 7.96 us
  starting transfers between devices: 34.9 us -> 11.8 us
  other arithmetic: 21.7 us -> 5.67 us
  between operations: 14.1 us -> 0.73 us
    pallas_call x0 -> x2, Pallas kernels: none -> 153 us  [the longest x1 144 us: lanczos(): pl.pallas_call(functools.partial(main_kernel, dims), out_shape=(jax.Shape...]
    psum x4 -> x0, blocking collectives: 133 us -> none  [gram_sums(): return lax.psum(values, 'wide')]
    psum x3 -> x0, waiting for transfers between devices: 91.8 us -> none  [per_device(): summed_blocks = lax.psum(summed_blocks, 'narrow')]
    dot_general x46 -> x0, matrix products: 78.5 us -> none  [the longest x6 28.5 us: tile_terms(): jnp.einsum('pab,prb->pra', kernel_values, second_vec, precision=HIGH)]
    all_to_all x6 -> x0, waiting for transfers between devices: 52.3 us -> none  [the longest x3 29.2 us: per_device(): lax.all_to_all(to_second.reshape(wide_count, capacity, vec_rows * BS), 'w...]
    all_to_all x6 -> x0, starting transfers between devices: 22.8 us -> none  [the longest x3 12 us: per_device(): lax.all_to_all(rows[local_ids], 'wide', split_axis=0, concat_axis=0, tile...]
    gather x12 -> x2, local copies, waits for them, and re-layouts: 20.7 us -> 1.11 us  [the longest x1 0.56 us: per_device(): first = first_rows[(me - turn) % wide_count].reshape(pair_count)]
    another operation x25 -> x0, other arithmetic: 16.5 us -> none  [the longest x9 6.38 us: per_device(): factor = jnp.linalg.cholesky(gram)]
  transfers between devices with their start and end apart: 11 -> 2, of which waited for: 10 -> 2; matrix products, arithmetic and copies ran while one was open for 4% -> 2% of each run, Pallas kernels for 0% -> 0%
where the time goes in v1:
time: 273 us; the launch traced here: 272 us
  Pallas kernels  153 us (56%)
  waiting for transfers between devices  92.1 us (34%)
  starting transfers between devices  11.8 us (4%)
  local copies, waits for them, and re-layouts  7.96 us (3%)
  other arithmetic  5.67 us (2%)
    pallas_call x1, Pallas kernels, lanczos(): pl.pallas_call(functools.partial(main_kernel, dims), out_shape=(jax.Shape...  144 us
    all_to_all x1, waiting for transfers between devices, per_device(): lax.all_to_all(unit[local_ids], 'wide', split_axis=0, concat_axis=0, tile...  89.9 us
    pallas_call x1, Pallas kernels, make_tiles(): pl.pallas_call(functools.partial(tiles_kernel, capacity), grid_spec=spec,...  8.98 us
    all_to_all x1, starting transfers between devices, per_device(): lax.all_to_all(wanted, 'wide', split_axis=0, concat_axis=0, tiled=True)  7.28 us
  transfers between devices with their start and end apart: 2, of which 2 were waited for; matrix products, arithmetic and copies ran while one was open for 2% of the time, Pallas kernels for 0%

profile of v1, /device:TPU:0, one launch (start us, length us, event | category | flops | bytes accessed | tf_op | source)
XLA Modules:
  0.0 271.7 jit_solution(13821968100012923628)
XLA Ops:
  0.6 0.8 slice_reduce_fusion
  1.4 0.7 all_to_all.9
  2.1 7.3 %all-to-all-start = ((s32[8,1,8]{2,1,0:T(1,128)}), s32[8,1,8]{2,1,0:T(1,128)S(1)}, u32[]{:S(2)}, u32[]{:S(2)}) async-start(s32[8,1,8]{2,1,0:T(1,128)} %bitcast.1), calls=%async_computation | async-start | bytes 8192 | tf_op jit(solution)/shard_map/all_to_all | solution.py:339
  9.4 2.2 fusion
  11.6 1.9 fusion.1
  13.5 0.0 copy-start
  13.6 2.2 all-to-all-done
  15.8 0.1 reshape.173
  15.9 2.8 %gather_fusion.2 = bf16[64,128,256]{2,1,0:T(8,128)(2,1)} fusion(bf16[32,128,256]{2,1,0:T(8,128)(2,1)S(1)} %bitcast.15, s32[1024]{0:T(1024)S(1)} %pad_clamp_fusion), kind=kCustom, calls=%fused_computation.2 | custom fusion | bytes 8388864 | tf_op jit(solution)/shard_map/gather | solution.py:341
  18.6 0.0 copy-done
  18.6 4.5 %all-to-all-start.1 = ((bf16[8,8,128,256]{3,2,1,0:T(8,128)(2,1)}), bf16[8,8,128,256]{3,2,1,0:T(8,128)(2,1)}, u32[]{:S(2)}, u32[]{:S(2)}) async-start(bf16[8,8,128,256]{3,2,1,0:T(8,128)(2,1)} %bitcast.17), calls=%async_computation.1 | async-start | bytes 8388608 | tf_op jit(solution)/shard_map/all_to_all | solution.py:341
  23.2 0.1 sub.44
  23.3 0.6 gather_fusion
  23.9 0.1 reshape.151.first_ref.first
  23.9 0.0 copy-start.1
  24.0 0.6 gather_fusion.1
  24.5 0.1 reshape.152.local
  24.6 0.0 copy-start.2
  24.6 0.1 pad_add_fusion
  24.7 0.6 fusion.2.owners
  25.3 89.9 %all-to-all-done.1.second_ref = bf16[8,8,128,256]{3,2,1,0:T(8,128)(2,1)} async-done(((bf16[8,8,128,256]{3,2,1,0:T(8,128)(2,1)}), bf16[8,8,128,256]{3,2,1,0:T(8,128)(2,1)}, u32[]{:S(2)}, u32[]{:S(2)}) %all-to-all-start.1) | async-done | bytes 4194336 | tf_op jit(solution)/shard_map/all_to_all | solution.py:341
  115.2 0.0 copy-done.1
  115.2 9.0 %tiles.1 = bf16[64,128,256]{2,1,0:T(8,128)(2,1)} custom-call(s32[1]{0:T(128)} %bitcast.5.me_ref, s32[64]{0:T(128)} %copy-done.1, bf16[32,128,256]{2,1,0:T(8,128)(2,1)} %bitcast.16, bf16[8,8,128,256]{3,2,1,0:T(8,128)(2,1)} %all-to-all-done.1.second_ref), custom_call_target="tpu_custom_call" | custom-call | tf_op jit(solution)/shard_map/tiles/pallas_call | solution.py:63
  124.2 0.0 copy-done.2
  124.2 144.4 %lanczos.1 = (f32[16,4096]{1,0:T(8,128)}, f32[3,2,16,16]{3,2,1,0:T(8,128)}) custom-call(s32[64]{0:T(128)} %copy-done.1, s32[64]{0:T(128)} %copy-done.2, bf16[32,256]{1,0:T(8,128)(2,1)} %fusion.2.owners, bf16[64,128,256]{2,1,0:T(8,128)(2,1)} %tiles.1, f32[16,4096]{1,0:T(8,128)} %q_ref.1), custom_call_target="tpu_custom_call" | custom-call | tf_op jit(solution)/shard_map/lanczos/pallas_call | solution.py:299
  268.7 1.7 copy.9
  270.3 1.4 copy.10
  (8 shorter events, 0.1 us)
Async XLA Ops:
  2.1 13.7 %all-to-all-start = ((s32[8,1,8]{2,1,0:T(1,128)}), s32[8,1,8]{2,1,0:T(1,128)S(1)}, u32[]{:S(2)}, u32[]{:S(2)}) async-start(s32[8,1,8]{2,1,0:T(1,128)} %bitcast.1), calls=%async_computation | async-start | bytes 8192 | tf_op jit(solution)/shard_map/all_to_all | solution.py:339
  13.5 5.1 %copy-start = (bf16[4096,256]{1,0:T(8,128)(2,1)}, bf16[4096,256]{1,0:T(8,128)(2,1)S(1)}, u32[]{:S(2)}) copy-start(bf16[4096,256]{1,0:T(8,128)(2,1)S(1)} %fusion.1) | copy-start | bytes 6291460
  18.6 96.6 %all-to-all-start.1 = ((bf16[8,8,128,256]{3,2,1,0:T(8,128)(2,1)}), bf16[8,8,128,256]{3,2,1,0:T(8,128)(2,1)}, u32[]{:S(2)}, u32[]{:S(2)}) async-start(bf16[8,8,128,256]{3,2,1,0:T(8,128)(2,1)} %bitcast.17), calls=%async_computation.1 | async-start | bytes 8388608 | tf_op jit(solution)/shard_map/all_to_all | solution.py:341
  23.9 91.3 %copy-start.1 = (s32[64]{0:T(128)}, s32[64]{0:T(128)S(1)}, u32[]{:S(2)}) copy-start(s32[64]{0:T(128)S(1)} %reshape.151.first_ref.first) | copy-start | bytes 772
  24.6 99.6 %copy-start.2 = (s32[64]{0:T(128)}, s32[64]{0:T(128)S(1)}, u32[]{:S(2)}) copy-start(s32[64]{0:T(128)S(1)} %reshape.152.local) | copy-start | bytes 772

commit v2 on v1

--- a/solution.py
+++ b/solution.py
@@ -281,6 +281,187 @@
 
     lax.fori_loop(0, STEPS, step, 0)
     out[...] = xs[:R, :]
+
+
+def spread_kernel(dims, first, second, asked, unit, tiles, *scratch):
+    W, N, C, B = dims
+    Z = W // 2
+    reach = Z - 1
+    bufs = (scratch[:reach], scratch[reach : 2 * reach])
+    out_buf, in_buf, sz, rz, sy, ry, sc, rc, sx, rx = scratch[2 * reach :]
+    me = lax.axis_index("wide")
+    nar = lax.axis_index("narrow")
+    z, x = lax.div(me, 2), lax.rem(me, 2)
+    across = me + 1 - 2 * x
+    over = lax.rem(nar + 2, N)
+    core = nar + 1 - 2 * lax.rem(nar, 2)
+    core_over = lax.rem(core + 2, N)
+    BQ = B // N
+
+    def valid(t, g):
+        return (z >= t) if g == 0 else (z + t < Z)
+
+    def room(g):
+        return (z + 1 < Z) if g == 0 else (z > 0)
+
+    def held(t, g):
+        return unit if t == 0 else bufs[g][t - 1]
+
+    def quarter(ref, q):
+        return ref.at[pl.ds(q * BQ, BQ)]
+
+    def remote(src, dst, send, recv, where):
+        return pltpu.make_async_remote_copy(
+            src_ref=src, dst_ref=dst, send_sem=send, recv_sem=recv,
+            device_id=where, device_id_type=MESH,
+        )
+
+    def along(t, g):
+        return remote(
+            quarter(held(t, g), nar), quarter(held(t + 1, g), nar),
+            sz.at[g, t], rz.at[g, t + 1], {"wide": me + 2 if g == 0 else me - 2},
+        )
+
+    def arrived(t, g):
+        part = quarter(held(t, g), nar)
+        return remote(
+            part, part, sz.at[g, t - 1], rz.at[g, t], {"wide": me + 2 if g == 0 else me - 2}
+        )
+
+    def sideways(t, g, q):
+        part = quarter(held(t, g), q)
+        return remote(part, part, sy.at[g, t], ry.at[g, t], {"narrow": over})
+
+    def inside(t, g, j, q):
+        part = quarter(held(t, g), q)
+        return remote(part, part, sc.at[j, g, t], rc.at[j, g, t], {"narrow": core})
+
+    def place(t, g):
+        return g * reach + t
+
+    def cross(t, g):
+        k = place(t, g)
+        return remote(out_buf.at[k], in_buf.at[k], sx.at[k], rx.at[k], {"wide": across})
+
+    def group_of(t, g):
+        return z - t if g == 0 else z + t
+
+    def serve(t, g):
+        o = 2 * group_of(t, g) + x
+        for c in range(C):
+            out_buf[place(t, g), c] = held(t, g)[asked[o * C + c]]
+        cross(t, g).start()
+
+    def make(o, load):
+        slot = lax.rem(me - o + W, W)
+        for c in range(C):
+            s = dot_nt(unit[first[slot * C + c]], load(o, c))
+            high, low = split(jnp.exp(KERNEL_FACTOR * (s - 1.0)))
+            tiles[slot * C + c, :, :BS] = high
+            tiles[slot * C + c, :, BS:] = low
+
+    def near_tiles(t, g):
+        make(2 * group_of(t, g) + x, lambda o, c: held(t, g)[second[o * C + c]])
+
+    def far_tiles(t, g):
+        cross(t, g).wait_recv()
+        make(2 * group_of(t, g) + 1 - x, lambda o, c: in_buf[place(t, g), c])
+
+    barrier = pltpu.get_barrier_semaphore()
+    for where in ({"wide": across}, {"narrow": over}, {"narrow": core}):
+        pl.semaphore_signal(barrier, inc=1, device_id=where, device_id_type=MESH)
+    for g in range(2):
+        @pl.when(room(g))
+        def _():
+            pl.semaphore_signal(
+                barrier, inc=1, device_id={"wide": me + 2 if g == 0 else me - 2},
+                device_id_type=MESH,
+            )
+    pl.semaphore_wait(barrier, 3 + jnp.minimum(z, 1) + jnp.minimum(Z - 1 - z, 1))
+
+    for g in range(2):
+        @pl.when(room(g))
+        def _():
+            along(0, g).start()
+    serve(0, 0)
+    near_tiles(0, 0)
+
+    for t in range(1, Z + 1):
+        if t < Z:
+            for g in range(2):
+                @pl.when(valid(t, g))
+                def _():
+                    arrived(t, g).wait_recv()
+
+                    @pl.when(room(g))
+                    def _():
+                        if t + 1 < Z:
+                            along(t, g).start()
+
+                    sideways(t, g, nar).start()
+                    inside(t, g, 0, nar).start()
+        if t > 1:
+            for g in range(2):
+                @pl.when(valid(t - 1, g))
+                def _():
+                    sideways(t - 1, g, over).wait_recv()
+                    inside(t - 1, g, 1, over).start()
+                    inside(t - 1, g, 0, core).wait_recv()
+                    inside(t - 1, g, 1, core_over).wait_recv()
+                    serve(t - 1, g)
+            for g in range(2):
+                @pl.when(valid(t - 1, g))
+                def _():
+                    near_tiles(t - 1, g)
+            if t == 2:
+                far_tiles(0, 0)
+    for t in range(1, Z):
+        for g in range(2):
+            @pl.when(valid(t, g))
+            def _():
+                far_tiles(t, g)
+
+    cross(0, 0).wait_send()
+    for t in range(Z):
+        for g in range(2):
+            if t:
+                @pl.when(valid(t, g))
+                def _():
+                    sideways(t, g, nar).wait_send()
+                    inside(t, g, 0, nar).wait_send()
+                    inside(t, g, 1, over).wait_send()
+                    cross(t, g).wait_send()
+
+            if t + 1 < Z:
+                @pl.when(valid(t, g) & room(g))
+                def _():
+                    along(t, g).wait_send()
+
+
+def spread_tiles(first, second, asked, unit, wide_count, narrow_count):
+    own_blocks, _, width = unit.shape
+    pair_count = first.shape[0]
+    C = pair_count // wide_count
+    Z = wide_count // 2
+    vmem = pl.BlockSpec(memory_space=pltpu.VMEM)
+    smem = pl.BlockSpec(memory_space=pltpu.SMEM)
+    half = pltpu.SemaphoreType.DMA((2, Z))
+    full = pltpu.SemaphoreType.DMA((2, 2, Z))
+    flat = pltpu.SemaphoreType.DMA((2 * Z - 1,))
+    ends = pltpu.VMEM((2 * Z - 1, C, BS, width), jnp.bfloat16)
+    return pl.pallas_call(
+        functools.partial(spread_kernel, (wide_count, narrow_count, C, own_blocks)),
+        out_shape=jax.ShapeDtypeStruct((pair_count, BS, 2 * BS), jnp.bfloat16),
+        in_specs=[smem, smem, smem, vmem],
+        out_specs=vmem,
+        scratch_shapes=[pltpu.VMEM(unit.shape, jnp.bfloat16)] * (2 * Z - 2)
+        + [ends, ends, half, half, half, half, full, full, flat, flat],
+        compiler_params=pltpu.CompilerParams(collective_id=1, has_side_effects=True),
+        name="spread",
+    )(first, second, asked, unit)
+
+
+SPREAD_BYTES = 16 * 2**20
 
 
 def lanczos(first, local, owners, tiles, q_init, wide_count, narrow_count, total):
@@ -334,20 +515,32 @@
     capacity = pair_count // wide_count
     total = own_blocks * BS * wide_count
     unit = unit_rows(points).reshape(own_blocks, BS, width)
-    wanted = pairs[1].reshape(wide_count, capacity)
-    local_ids = (
-        lax.all_to_all(wanted, "wide", split_axis=0, concat_axis=0, tiled=True) - me * own_blocks
-    )
-    second = lax.all_to_all(unit[local_ids], "wide", split_axis=0, concat_axis=0, tiled=True)
     turn = jnp.arange(wide_count, dtype=jnp.int32)
     first_rows = (pairs[0] - me * own_blocks).reshape(wide_count, capacity)
     first = first_rows[(me - turn) % wide_count].reshape(pair_count)
-    local = local_ids.reshape(wide_count, capacity)[(me + turn) % wide_count].reshape(pair_count)
+    second = (pairs[1].reshape(wide_count, capacity) - turn[:, None] * own_blocks)
+    every = lax.all_to_all(
+        jnp.broadcast_to(second.reshape(1, pair_count), (wide_count, pair_count)),
+        "wide", split_axis=0, concat_axis=0, tiled=True,
+    ).reshape(wide_count, wide_count, capacity)
+    local_ids = lax.dynamic_index_in_dim(every, me, axis=1, keepdims=False)
+    local = local_ids[(me + turn) % wide_count].reshape(pair_count)
     targets = jnp.concatenate([first, local, first, local])
     owners = (jnp.arange(own_blocks, dtype=jnp.int32)[:, None] == targets[None, :]).astype(
         jnp.bfloat16
     )
-    tiles = make_tiles(jnp.reshape(me, (1,)).astype(jnp.int32), first, unit, second.reshape(wide_count, capacity, BS, width))
+    buffers = (wide_count - 2) * unit.size * 2
+    if wide_count % 2 == 0 and wide_count > 2 and narrow_count == 4 and buffers <= SPREAD_BYTES:
+        asked = lax.dynamic_index_in_dim(every, me + 1 - 2 * (me % 2), axis=0, keepdims=False)
+        tiles = spread_tiles(
+            first, second.reshape(pair_count), asked.reshape(pair_count), unit,
+            wide_count, narrow_count,
+        )
+    else:
+        blocks = lax.all_to_all(
+            unit[local_ids.reshape(pair_count)], "wide", split_axis=0, concat_axis=0, tiled=True
+        ).reshape(wide_count, capacity, BS, width)
+        tiles = make_tiles(jnp.reshape(me, (1,)).astype(jnp.int32), first, unit, blocks)
     return lanczos(first, local, owners, tiles, q_init, wide_count, narrow_count, total)
 
 

time: 273 us -> 239 us (0.88)
  waiting for transfers between devices: 92.1 us -> 0.01 us
  Pallas kernels: 153 us -> 215 us
  starting transfers between devices: 11.8 us -> 7.28 us
  other arithmetic: 5.67 us -> 8.54 us
    all_to_all x2 -> x1, waiting for transfers between devices: 92.1 us -> 0.01 us  [per_device(): lax.all_to_all(jnp.broadcast_to(second.reshape(1, pair_count), (wide_coun...]
    pallas_call x1, Pallas kernels: 8.98 us -> 69.3 us  [spread_tiles(): pl.pallas_call(functools.partial(spread_kernel, (wide_count, narrow_count...]
    all_to_all x2 -> x1, starting transfers between devices: 11.8 us -> 7.28 us  [per_device(): lax.all_to_all(jnp.broadcast_to(second.reshape(1, pair_count), (wide_coun...]
    gather x2 -> x1, local copies, waits for them, and re-layouts: 3.31 us -> 0.55 us  [per_device(): local = local_ids[(me + turn) % wide_count].reshape(pair_count)]
  transfers between devices with their start and end apart: 2 -> 1, of which waited for: 2 -> 0; matrix products, arithmetic and copies ran while one was open for 2% -> 3% of each run, Pallas kernels for 0% -> 0%
where the time goes in v2:
time: 239 us
  Pallas kernels  215 us (90%)
  other arithmetic  8.54 us (4%)
  starting transfers between devices  7.28 us (3%)
  local copies, waits for them, and re-layouts  6.52 us (3%)
    pallas_call x1, Pallas kernels, lanczos(): pl.pallas_call(functools.partial(main_kernel, dims), out_shape=(jax.Shape...  146 us
    pallas_call x1, Pallas kernels, spread_tiles(): pl.pallas_call(functools.partial(spread_kernel, (wide_count, narrow_count...  69.3 us
    all_to_all x1, starting transfers between devices, per_device(): lax.all_to_all(jnp.broadcast_to(second.reshape(1, pair_count), (wide_coun...  7.28 us
  transfers between devices with their start and end apart: 1, of which 0 were waited for; matrix products, arithmetic and copies ran while one was open for 3% of the time, Pallas kernels for 0%

profile of v2, /device:TPU:0, one launch (start us, length us, event | category | flops | bytes accessed | tf_op | source)
XLA Modules:
  0.0 238.5 jit_solution(2739181952134834939)
XLA Ops:
  0.6 0.1 sub.51
  0.7 0.1 sub.52
  0.8 0.8 subtract_bitcast_fusion
  1.6 0.6 broadcast_in_dim.2
  2.2 7.3 %all-to-all-start = ((s32[8,1,64]{2,1,0:T(1,128)}), s32[8,1,64]{2,1,0:T(1,128)S(1)}, u32[]{:S(2)}, u32[]{:S(2)}) async-start(s32[8,1,64]{2,1,0:T(1,128)} %broadcast_in_dim.2), calls=%async_computation | async-start | bytes 8192 | tf_op jit(solution)/shard_map/all_to_all | solution.py:522
  9.5 0.1 sub.55
  9.5 1.2 bitcast_subtract_fusion.second
  10.8 2.2 fusion
  13.0 2.9 %fusion.1 = bf16[4096,256]{1,0:T(8,128)(2,1)} fusion(bf16[4096,256]{1,0:T(8,128)(2,1)} %param.3, f32[4096]{0:T(1024)S(1)} %add_rsqrt_fusion), kind=kLoop, calls=%fused_computation.5 | loop fusion | flops 3145728 | bytes 4210688 | tf_op jit(solution)/shard_map/convert_element_type | solution.py:21
  15.9 0.1 sub.48
  16.0 0.6 gather_fusion
  16.6 0.1 reshape.148.first
  16.7 0.0 copy-start
  16.7 0.0 all-to-all-done
  16.7 0.5 broadcast.165
  17.2 0.7 reduce.7
  17.9 0.1 reshape.149
  17.9 0.7 reshape.151.asked
  18.6 0.6 gather_fusion.1
  19.2 0.1 reshape.150.local
  19.2 0.0 copy-start.1
  19.2 0.1 pad_add_fusion
  19.3 0.6 fusion.2.owners
  19.9 0.0 copy-done
  19.9 69.3 %spread.1.tiles = bf16[64,128,256]{2,1,0:T(8,128)(2,1)} custom-call(s32[64]{0:T(128)} %copy-done, s32[64]{0:T(128)} %bitcast_subtract_fusion.second, s32[64]{0:T(128)} %reshape.151.asked, bf16[32,128,256]{2,1,0:T(8,128)(2,1)} %bitcast.10), custom_call_target="tpu_custom_call" | custom-call | tf_op jit(solution)/shard_map/spread/pallas_call | solution.py:452
  89.3 0.0 copy-done.1
  89.3 146.1 %lanczos.1 = (f32[16,4096]{1,0:T(8,128)}, f32[3,2,16,16]{3,2,1,0:T(8,128)}) custom-call(s32[64]{0:T(128)} %copy-done, s32[64]{0:T(128)} %copy-done.1, bf16[32,256]{1,0:T(8,128)(2,1)} %fusion.2.owners, bf16[64,128,256]{2,1,0:T(8,128)(2,1)} %spread.1.tiles, f32[16,4096]{1,0:T(8,128)} %q_ref.1), custom_call_target="tpu_custom_call" | custom-call | tf_op jit(solution)/shard_map/lanczos/pallas_call | solution.py:480
  235.5 1.7 copy.7
  237.1 1.4 copy.8
  (7 shorter events, 0.0 us)
Async XLA Ops:
  2.2 14.5 %all-to-all-start = ((s32[8,1,64]{2,1,0:T(1,128)}), s32[8,1,64]{2,1,0:T(1,128)S(1)}, u32[]{:S(2)}, u32[]{:S(2)}) async-start(s32[8,1,64]{2,1,0:T(1,128)} %broadcast_in_dim.2), calls=%async_computation | async-start | bytes 8192 | tf_op jit(solution)/shard_map/all_to_all | solution.py:522
  16.7 3.3 %copy-start = (s32[64]{0:T(128)}, s32[64]{0:T(128)S(1)}, u32[]{:S(2)}) copy-start(s32[64]{0:T(128)S(1)} %reshape.148.first) | copy-start | bytes 772
  19.2 70.1 %copy-start.1 = (s32[64]{0:T(128)}, s32[64]{0:T(128)S(1)}, u32[]{:S(2)}) copy-start(s32[64]{0:T(128)S(1)} %reshape.150.local) | copy-start | bytes 772

commit v3 on v2

--- a/solution.py
+++ b/solution.py
@@ -9,6 +9,7 @@
 
 BS = 128
 STEPS = 3
+LEVELS = 32767.0
 KERNEL_FACTOR = 3.0
 EPSILON = 1e-06
 HIGH = lax.Precision.HIGHEST
@@ -24,6 +25,16 @@
 def split(x):
     high = x.astype(jnp.bfloat16)
     return high, (x - high.astype(jnp.float32)).astype(jnp.bfloat16)
+
+
+def coded(x):
+    top = jnp.maximum(jnp.max(jnp.abs(x), axis=1, keepdims=True), 1e-30)
+    scaled = jnp.clip(jnp.round(x * (LEVELS / top)), -LEVELS, LEVELS)
+    return scaled.astype(jnp.int32).astype(jnp.int16), top * (1.0 / LEVELS)
+
+
+def number(x):
+    return x.astype(jnp.int32).astype(jnp.float32)
 
 
 def dot32(a, b):
@@ -87,8 +98,8 @@
 
 def main_kernel(
     dims, first, local, owners, tiles, q_ref, out, coef,
-    sb, rb, sb2, rb2, tf, pb, rs, ag, xs, blocks, prev, up, gs, gr,
-    s1, r1, s2, r2, s3, r3, s4, r4, s5, r5,
+    sb, rb, sb2, rq, ss, rs1, ss2, rs2, coded_blocks, scales, rb2, tf, pb, rs, ag, xs, blocks, prev, up, gs, gr,
+    s1, r1, s2, r2, s3, r3, s4, r4, s5, r5, s6, r6, s7, r7,
 ):
     W, N, C, R, B, total = dims
     CR = C * R
@@ -122,9 +133,25 @@
     def answer(d):
         rows = pl.ds(d * CR, CR)
         return pltpu.make_async_remote_copy(
-            src_ref=sb2.at[rows], dst_ref=rb2.at[rows], send_sem=s2.at[d], recv_sem=r2.at[d],
+            src_ref=sb2.at[rows], dst_ref=rq.at[rows], send_sem=s2.at[d], recv_sem=r2.at[d],
             device_id={"wide": down_peer(d)}, device_id_type=MESH,
         )
+
+    def request_scale(d):
+        rows = pl.ds(d * R, R)
+        return pltpu.make_async_remote_copy(
+            src_ref=ss.at[rows], dst_ref=rs1.at[rows], send_sem=s6.at[d], recv_sem=r6.at[d],
+            device_id={"wide": up_peer(d)}, device_id_type=MESH,
+        )
+
+    def answer_scale(d):
+        rows = pl.ds(d * R, R)
+        return pltpu.make_async_remote_copy(
+            src_ref=ss2.at[rows], dst_ref=rs2.at[rows], send_sem=s7.at[d], recv_sem=r7.at[d],
+            device_id={"wide": down_peer(d)}, device_id_type=MESH,
+        )
+
+    lane = lax.broadcasted_iota(jnp.int32, (R, BS), 1)
 
     def scatter(d):
         return pltpu.make_async_remote_copy(
@@ -178,24 +205,36 @@
 
     def step(k, carry):
         for b in range(B):
-            blocks[b] = xs[:R, b * BS : (b + 1) * BS]
+            value = xs[:R, b * BS : (b + 1) * BS]
+            blocks[b] = value
+            whole, unit_of = coded(value)
+            coded_blocks[b] = whole
+            scales[b] = jnp.broadcast_to(unit_of, (R, BS))
         for d in range(W):
+            spread = jnp.zeros((R, BS), jnp.float32)
             for c in range(C):
-                value = blocks[local[d * C + c]]
+                value = coded_blocks[local[d * C + c]]
                 (rb if d == 0 else sb)[pl.ds((d * C + c) * R, R), :] = value
+                spread = jnp.where(lane == c, scales[local[d * C + c]], spread)
+            (rs1 if d == 0 else ss)[pl.ds(d * R, R), :] = spread
             if d:
                 request(d).start()
+                request_scale(d).start()
 
         def group(d, carry):
             @pl.when(d > 0)
             def _():
                 request(d).wait_recv()
-
+                request_scale(d).wait_recv()
+
+            scale_rows = pl.ds(pl.multiple_of(d * R, R), R)
+            scale = rs1[scale_rows, :]
+            spread = jnp.zeros((R, BS), jnp.float32)
             for c in range(C):
                 p = d * C + c
                 rows = pl.ds(pl.multiple_of(p * R, R), R)
                 tile = tiles[p]
-                high, low = split(rb[rows, :])
+                high, low = split(number(rb[rows, :]))
                 left = jnp.concatenate(
                     [
                         jnp.concatenate([high, high], axis=1),
@@ -204,23 +243,32 @@
                     axis=0,
                 )
                 both = dot_nt(left, tile)
-                tf[rows, :] = both[:R] + both[R:]
+                tf[rows, :] = (both[:R] + both[R:]) * scale[:, c : c + 1]
                 high, low = split(blocks[first[p]])
                 both = jnp.dot(
                     jnp.concatenate([high, low], axis=0), tile, preferred_element_type=jnp.float32
                 )
-                sb2[rows, :] = both[:R, :BS] + both[R:, :BS] + both[:R, BS:]
+                whole, unit_of = coded(both[:R, :BS] + both[R:, :BS] + both[:R, BS:])
+                sb2[rows, :] = whole
+                spread = jnp.where(lane == c, unit_of, spread)
+            ss2[scale_rows, :] = spread
 
             @pl.when(d > 0)
             def _():
                 answer(d).start()
+                answer_scale(d).start()
 
             return carry
 
         lax.fori_loop(0, W, group, 0)
-        rb2[pl.ds(0, CR), :] = sb2[pl.ds(0, CR), :]
-        for d in range(1, W):
-            answer(d).wait_recv()
+        for d in range(W):
+            if d:
+                answer(d).wait_recv()
+                answer_scale(d).wait_recv()
+            scale = (rs2 if d else ss2)[pl.ds(d * R, R), :]
+            for c in range(C):
+                rows = pl.ds((d * C + c) * R, R)
+                rb2[rows, :] = number((rq if d else sb2)[rows, :]) * scale[:, c : c + 1]
 
         one_hot = owners[...]
         for n in range(1, N + 1):
@@ -274,6 +322,8 @@
         for d in range(1, W):
             request(d).wait_send()
             answer(d).wait_send()
+            request_scale(d).wait_send()
+            answer_scale(d).wait_send()
         for d in range(1, N):
             scatter(d).wait_send()
             gather(d).wait_send()
@@ -474,6 +524,8 @@
     smem = pl.BlockSpec(memory_space=pltpu.SMEM)
     f32 = jnp.float32
     pairs_buf = pltpu.VMEM((pair_count * R, BS), f32)
+    coded_buf = pltpu.VMEM((pair_count * R, BS), jnp.int16)
+    scale_buf = pltpu.VMEM((wide_count * R, BS), f32)
     part = R // narrow_count * B
     wide_sem = pltpu.SemaphoreType.DMA((wide_count,))
     narrow_sem = pltpu.SemaphoreType.DMA((narrow_count,))
@@ -486,7 +538,11 @@
         in_specs=[smem, smem, vmem, vmem, vmem],
         out_specs=(vmem, vmem),
         scratch_shapes=[
-            pairs_buf, pairs_buf, pairs_buf, pairs_buf, pairs_buf,
+            coded_buf, coded_buf, coded_buf, coded_buf,
+            scale_buf, scale_buf, scale_buf, scale_buf,
+            pltpu.VMEM((B, R, BS), jnp.int16),
+            pltpu.VMEM((B, R, BS), f32),
+            pairs_buf, pairs_buf,
             pltpu.VMEM((R * B, BS), f32),
             pltpu.VMEM((narrow_count, part, BS), f32),
             pltpu.VMEM((R * B, BS), f32),
@@ -498,7 +554,7 @@
             pltpu.VMEM((wide_count, 2 * R, BS), f32),
             wide_sem, wide_sem, wide_sem, wide_sem,
             narrow_sem, narrow_sem, narrow_sem, narrow_sem,
-            wide_sem, wide_sem,
+            wide_sem, wide_sem, wide_sem, wide_sem, wide_sem, wide_sem,
         ],
         compiler_params=pltpu.CompilerParams(collective_id=0, has_side_effects=True),
         name="lanczos",

time: 239 us -> 211 us (0.88)
  Pallas kernels: 215 us -> 187 us
    pallas_call x1, Pallas kernels: 146 us -> 118 us  [lanczos(): pl.pallas_call(functools.partial(main_kernel, dims), out_shape=(jax.Shape...]
where the time goes in v3:
time: 211 us; the launch traced here: 210 us
  Pallas kernels  187 us (89%)
  other arithmetic  8.54 us (4%)
  starting transfers between devices  7.28 us (3%)
  local copies, waits for them, and re-layouts  6.52 us (3%)
    pallas_call x1, Pallas kernels, lanczos(): pl.pallas_call(functools.partial(main_kernel, dims), out_shape=(jax.Shape...  118 us
    pallas_call x1, Pallas kernels, spread_tiles(): pl.pallas_call(functools.partial(spread_kernel, (wide_count, narrow_count...  69.3 us
    all_to_all x1, starting transfers between devices, per_device(): lax.all_to_all(jnp.broadcast_to(second.reshape(1, pair_count), (wide_coun...  7.28 us
  transfers between devices with their start and end apart: 1, of which 0 were waited for; matrix products, arithmetic and copies ran while one was open for 3% of the time, Pallas kernels for 0%

profile of v3, /device:TPU:0, one launch (start us, length us, event | category | flops | bytes accessed | tf_op | source)
XLA Modules:
  0.0 210.3 jit_solution(2575056108678900641)
XLA Ops:
  0.6 0.1 sub.51
  0.7 0.1 sub.52
  0.8 0.8 subtract_bitcast_fusion
  1.6 0.6 broadcast_in_dim.2
  2.2 7.3 %all-to-all-start = ((s32[8,1,64]{2,1,0:T(1,128)}), s32[8,1,64]{2,1,0:T(1,128)S(1)}, u32[]{:S(2)}, u32[]{:S(2)}) async-start(s32[8,1,64]{2,1,0:T(1,128)} %broadcast_in_dim.2), calls=%async_computation | async-start | bytes 8192 | tf_op jit(solution)/shard_map/all_to_all | solution.py:578
  9.5 0.1 sub.55
  9.5 1.2 bitcast_subtract_fusion.second
  10.8 2.2 %fusion = f32[4096]{0:T(1024)S(1)} fusion(bf16[4096,256]{1,0:T(8,128)(2,1)} %param.3), kind=kLoop, calls=%fused_computation.4 | loop fusion | flops 3141632 | bytes 2113536 | tf_op jit(solution)/shard_map/reduce_sum | solution.py:21
  13.0 2.9 %fusion.1 = bf16[4096,256]{1,0:T(8,128)(2,1)} fusion(bf16[4096,256]{1,0:T(8,128)(2,1)} %param.3, f32[4096]{0:T(1024)S(1)} %add_rsqrt_fusion), kind=kLoop, calls=%fused_computation.5 | loop fusion | flops 3145728 | bytes 4210688 | tf_op jit(solution)/shard_map/convert_element_type | solution.py:22
  15.9 0.1 sub.48
  16.0 0.6 gather_fusion
  16.6 0.1 reshape.148.first
  16.7 0.0 copy-start
  16.7 0.0 all-to-all-done
  16.7 0.5 broadcast.165
  17.2 0.7 reduce.7
  17.9 0.1 reshape.149
  17.9 0.7 reshape.151.asked
  18.6 0.6 gather_fusion.1
  19.2 0.1 reshape.150.local
  19.2 0.0 copy-start.1
  19.2 0.1 pad_add_fusion
  19.3 0.6 fusion.2.owners
  19.9 0.0 copy-done
  19.9 69.3 %spread.1.tiles = bf16[64,128,256]{2,1,0:T(8,128)(2,1)} custom-call(s32[64]{0:T(128)} %copy-done, s32[64]{0:T(128)} %bitcast_subtract_fusion.second, s32[64]{0:T(128)} %reshape.151.asked, bf16[32,128,256]{2,1,0:T(8,128)(2,1)} %bitcast.10), custom_call_target="tpu_custom_call" | custom-call | tf_op jit(solution)/shard_map/spread/pallas_call | solution.py:502
  89.3 0.0 copy-done.1
  89.3 117.9 %lanczos.1 = (f32[16,4096]{1,0:T(8,128)}, f32[3,2,16,16]{3,2,1,0:T(8,128)}) custom-call(s32[64]{0:T(128)} %copy-done, s32[64]{0:T(128)} %copy-done.1, bf16[32,256]{1,0:T(8,128)(2,1)} %fusion.2.owners, bf16[64,128,256]{2,1,0:T(8,128)(2,1)} %spread.1.tiles, f32[16,4096]{1,0:T(8,128)} %q_ref.1), custom_call_target="tpu_custom_call" | custom-call | tf_op jit(solution)/shard_map/lanczos/pallas_call | solution.py:532
  207.2 1.7 copy.7
  208.9 1.4 copy.8
  (7 shorter events, 0.0 us)
Async XLA Ops:
  2.2 14.5 %all-to-all-start = ((s32[8,1,64]{2,1,0:T(1,128)}), s32[8,1,64]{2,1,0:T(1,128)S(1)}, u32[]{:S(2)}, u32[]{:S(2)}) async-start(s32[8,1,64]{2,1,0:T(1,128)} %broadcast_in_dim.2), calls=%async_computation | async-start | bytes 8192 | tf_op jit(solution)/shard_map/all_to_all | solution.py:578
  16.7 3.3 %copy-start = (s32[64]{0:T(128)}, s32[64]{0:T(128)S(1)}, u32[]{:S(2)}) copy-start(s32[64]{0:T(128)S(1)} %reshape.148.first) | copy-start | bytes 772
  19.2 70.1 %copy-start.1 = (s32[64]{0:T(128)}, s32[64]{0:T(128)S(1)}, u32[]{:S(2)}) copy-start(s32[64]{0:T(128)S(1)} %reshape.150.local) | copy-start | bytes 772

commit v4 on v3

--- a/solution.py
+++ b/solution.py
@@ -27,8 +27,8 @@
     return high, (x - high.astype(jnp.float32)).astype(jnp.bfloat16)
 
 
-def coded(x):
-    top = jnp.maximum(jnp.max(jnp.abs(x), axis=1, keepdims=True), 1e-30)
+def coded(x, axes=1):
+    top = jnp.maximum(jnp.max(jnp.abs(x), axis=axes, keepdims=True), 1e-30)
     scaled = jnp.clip(jnp.round(x * (LEVELS / top)), -LEVELS, LEVELS)
     return scaled.astype(jnp.int32).astype(jnp.int16), top * (1.0 / LEVELS)
 
@@ -98,8 +98,8 @@
 
 def main_kernel(
     dims, first, local, owners, tiles, q_ref, out, coef,
-    sb, rb, sb2, rq, ss, rs1, ss2, rs2, coded_blocks, scales, rb2, tf, pb, rs, ag, xs, blocks, prev, up, gs, gr,
-    s1, r1, s2, r2, s3, r3, s4, r4, s5, r5, s6, r6, s7, r7,
+    sb, rb, sb2, rq, ss, rs1, ss2, rs2, coded_blocks, scales, rb2, tf, pb, rs, ag, acc, out16, all16, psc, rsc, osc, asc, xs, blocks, prev, up, gs, gr,
+    s1, r1, s2, r2, s3, r3, s4, r4, s5, r5, s6, r6, s7, r7, s8, r8, s9, r9,
 ):
     W, N, C, R, B, total = dims
     CR = C * R
@@ -163,16 +163,30 @@
     def gather(d):
         mine = pl.ds(nar * PR, PR)
         return pltpu.make_async_remote_copy(
-            src_ref=rs.at[0], dst_ref=ag.at[mine], send_sem=s4.at[d], recv_sem=r4.at[d],
+            src_ref=out16, dst_ref=all16.at[mine], send_sem=s4.at[d], recv_sem=r4.at[d],
             device_id={"narrow": lax.rem(nar + d, N)}, device_id_type=MESH,
         )
 
     def gathered(d):
         theirs = pl.ds(lax.rem(nar - d + N, N) * PR, PR)
         return pltpu.make_async_remote_copy(
-            src_ref=rs.at[0], dst_ref=ag.at[theirs], send_sem=s4.at[d], recv_sem=r4.at[d],
+            src_ref=out16, dst_ref=all16.at[theirs], send_sem=s4.at[d], recv_sem=r4.at[d],
             device_id={"narrow": lax.rem(nar + d, N)}, device_id_type=MESH,
         )
+
+    def scatter_scale(d):
+        return pltpu.make_async_remote_copy(
+            src_ref=psc.at[d], dst_ref=rsc.at[d], send_sem=s8.at[d], recv_sem=r8.at[d],
+            device_id={"narrow": lax.rem(nar + d, N)}, device_id_type=MESH,
+        )
+
+    def gather_scale(d, slot):
+        return pltpu.make_async_remote_copy(
+            src_ref=osc, dst_ref=asc.at[slot], send_sem=s9.at[d], recv_sem=r9.at[d],
+            device_id={"narrow": lax.rem(nar + d, N)}, device_id_type=MESH,
+        )
+
+    lane8 = lax.broadcasted_iota(jnp.int32, (8, BS), 1)
 
     def gram_copy(d):
         return pltpu.make_async_remote_copy(
@@ -273,6 +287,7 @@
         one_hot = owners[...]
         for n in range(1, N + 1):
             part = lax.rem(nar + n, N)
+            spread = jnp.zeros((8, BS), jnp.float32)
             for q in range(RN):
                 r = part * RN + q
                 x = jnp.concatenate(
@@ -285,22 +300,40 @@
                     preferred_element_type=jnp.float32,
                 )
                 if n == N:
-                    rs[0, pl.ds(q * B, B), :] = value
+                    acc[pl.ds(q * B, B), :] = value
                 else:
-                    pb[pl.ds(pl.multiple_of(part * PR + q * B, B), B), :] = value
+                    whole, unit_of = coded(value, (0, 1))
+                    pb[pl.ds(pl.multiple_of(part * PR + q * B, B), B), :] = whole
+                    spread = jnp.where(lane8 == q, unit_of, spread)
             if n < N:
+                psc[n] = spread
                 scatter(n).start()
+                scatter_scale(n).start()
         for d in range(1, N):
             scatter(d).wait_recv()
-        mine = rs[0]
-        for d in range(1, N):
-            mine += rs[d]
-        rs[0] = mine
+            scatter_scale(d).wait_recv()
+        spread = jnp.zeros((8, BS), jnp.float32)
+        for q in range(RN):
+            rows = pl.ds(q * B, B)
+            value = acc[rows, :]
+            for d in range(1, N):
+                value += number(rs[d, rows, :]) * rsc[d][:1, q : q + 1]
+            whole, unit_of = coded(value, (0, 1))
+            out16[rows, :] = whole
+            all16[pl.ds(pl.multiple_of(nar * PR + q * B, B), B), :] = whole
+            spread = jnp.where(lane8 == q, unit_of, spread)
+        osc[...] = spread
+        asc[nar] = spread
         for d in range(1, N):
             gather(d).start()
-        ag[pl.ds(pl.multiple_of(nar * PR, PR), PR), :] = mine
+            gather_scale(d, nar).start()
         for d in range(1, N):
             gathered(d).wait_recv()
+            gather_scale(d, lax.rem(nar - d + N, N)).wait_recv()
+        for r in range(R):
+            rows = pl.ds(r * B, B)
+            unit_of = asc[r // RN][:1, r % RN : r % RN + 1]
+            ag[rows, :] = number(all16[rows, :]) * unit_of
 
         for b in range(B):
             xs[R:, b * BS : (b + 1) * BS] = ag[pl.ds(b, R, stride=B), :]
@@ -327,6 +360,8 @@
         for d in range(1, N):
             scatter(d).wait_send()
             gather(d).wait_send()
+            scatter_scale(d).wait_send()
+            gather_scale(d, nar).wait_send()
         return carry
 
     lax.fori_loop(0, STEPS, step, 0)
@@ -543,9 +578,16 @@
             pltpu.VMEM((B, R, BS), jnp.int16),
             pltpu.VMEM((B, R, BS), f32),
             pairs_buf, pairs_buf,
+            pltpu.VMEM((R * B, BS), jnp.int16),
+            pltpu.VMEM((narrow_count, part, BS), jnp.int16),
             pltpu.VMEM((R * B, BS), f32),
-            pltpu.VMEM((narrow_count, part, BS), f32),
-            pltpu.VMEM((R * B, BS), f32),
+            pltpu.VMEM((part, BS), f32),
+            pltpu.VMEM((part, BS), jnp.int16),
+            pltpu.VMEM((R * B, BS), jnp.int16),
+            pltpu.VMEM((narrow_count, 8, BS), f32),
+            pltpu.VMEM((narrow_count, 8, BS), f32),
+            pltpu.VMEM((8, BS), f32),
+            pltpu.VMEM((narrow_count, 8, BS), f32),
             pltpu.VMEM((2 * R, cols), f32),
             pltpu.VMEM((B, R, BS), f32),
             pltpu.VMEM((R, cols), f32),
@@ -555,6 +597,7 @@
             wide_sem, wide_sem, wide_sem, wide_sem,
             narrow_sem, narrow_sem, narrow_sem, narrow_sem,
             wide_sem, wide_sem, wide_sem, wide_sem, wide_sem, wide_sem,
+            narrow_sem, narrow_sem, narrow_sem, narrow_sem,
         ],
         compiler_params=pltpu.CompilerParams(collective_id=0, has_side_effects=True),
         name="lanczos",

time: 211 us -> 209 us (level)
  no operation moved by 1% of the time
where the time goes in v4:
time: 209 us
  Pallas kernels  186 us (89%)
  other arithmetic  8.54 us (4%)
  starting transfers between devices  7.28 us (3%)
  local copies, waits for them, and re-layouts  6.52 us (3%)
    pallas_call x1, Pallas kernels, lanczos(): pl.pallas_call(functools.partial(main_kernel, dims), out_shape=(jax.Shape...  116 us
    pallas_call x1, Pallas kernels, spread_tiles(): pl.pallas_call(functools.partial(spread_kernel, (wide_count, narrow_count...  69.3 us
    all_to_all x1, starting transfers between devices, per_device(): lax.all_to_all(jnp.broadcast_to(second.reshape(1, pair_count), (wide_coun...  7.28 us
  transfers between devices with their start and end apart: 1, of which 0 were waited for; matrix products, arithmetic and copies ran while one was open for 3% of the time, Pallas kernels for 0%

profile of v4, /device:TPU:0, one launch (start us, length us, event | category | flops | bytes accessed | tf_op | source)
XLA Modules:
  0.0 208.7 jit_solution(14898750855892094826)
XLA Ops:
  0.6 0.1 sub.51
  0.7 0.1 sub.52
  0.8 0.8 subtract_bitcast_fusion
  1.6 0.6 broadcast_in_dim.2
  2.2 7.3 %all-to-all-start = ((s32[8,1,64]{2,1,0:T(1,128)}), s32[8,1,64]{2,1,0:T(1,128)S(1)}, u32[]{:S(2)}, u32[]{:S(2)}) async-start(s32[8,1,64]{2,1,0:T(1,128)} %broadcast_in_dim.2), calls=%async_computation | async-start | bytes 8192 | tf_op jit(solution)/shard_map/all_to_all | solution.py:621
  9.5 0.1 sub.55
  9.5 1.2 bitcast_subtract_fusion.second
  10.8 2.2 %fusion = f32[4096]{0:T(1024)S(1)} fusion(bf16[4096,256]{1,0:T(8,128)(2,1)} %param.3), kind=kLoop, calls=%fused_computation.4 | loop fusion | flops 3141632 | bytes 2113536 | tf_op jit(solution)/shard_map/reduce_sum | solution.py:21
  13.0 2.9 %fusion.1 = bf16[4096,256]{1,0:T(8,128)(2,1)} fusion(bf16[4096,256]{1,0:T(8,128)(2,1)} %param.3, f32[4096]{0:T(1024)S(1)} %add_rsqrt_fusion), kind=kLoop, calls=%fused_computation.5 | loop fusion | flops 3145728 | bytes 4210688 | tf_op jit(solution)/shard_map/convert_element_type | solution.py:22
  15.9 0.1 sub.48
  16.0 0.6 gather_fusion
  16.6 0.1 reshape.148.first
  16.7 0.0 copy-start
  16.7 0.0 all-to-all-done
  16.7 0.5 broadcast.165
  17.2 0.7 reduce.7
  17.9 0.1 reshape.149
  17.9 0.7 reshape.151.asked
  18.6 0.6 gather_fusion.1
  19.2 0.1 reshape.150.local
  19.2 0.0 copy-start.1
  19.2 0.1 pad_add_fusion
  19.3 0.6 fusion.2.owners
  19.9 0.0 copy-done
  19.9 69.3 %spread.1.tiles = bf16[64,128,256]{2,1,0:T(8,128)(2,1)} custom-call(s32[64]{0:T(128)} %copy-done, s32[64]{0:T(128)} %bitcast_subtract_fusion.second, s32[64]{0:T(128)} %reshape.151.asked, bf16[32,128,256]{2,1,0:T(8,128)(2,1)} %bitcast.10), custom_call_target="tpu_custom_call" | custom-call | tf_op jit(solution)/shard_map/spread/pallas_call | solution.py:537
  89.3 0.0 copy-done.1
  89.3 116.3 %lanczos.1 = (f32[16,4096]{1,0:T(8,128)}, f32[3,2,16,16]{3,2,1,0:T(8,128)}) custom-call(s32[64]{0:T(128)} %copy-done, s32[64]{0:T(128)} %copy-done.1, bf16[32,256]{1,0:T(8,128)(2,1)} %fusion.2.owners, bf16[64,128,256]{2,1,0:T(8,128)(2,1)} %spread.1.tiles, f32[16,4096]{1,0:T(8,128)} %q_ref.1), custom_call_target="tpu_custom_call" | custom-call | tf_op jit(solution)/shard_map/lanczos/pallas_call | solution.py:567
  205.6 1.7 copy.7
  207.2 1.4 copy.8
  (7 shorter events, 0.0 us)
Async XLA Ops:
  2.2 14.5 %all-to-all-start = ((s32[8,1,64]{2,1,0:T(1,128)}), s32[8,1,64]{2,1,0:T(1,128)S(1)}, u32[]{:S(2)}, u32[]{:S(2)}) async-start(s32[8,1,64]{2,1,0:T(1,128)} %broadcast_in_dim.2), calls=%async_computation | async-start | bytes 8192 | tf_op jit(solution)/shard_map/all_to_all | solution.py:621
  16.7 3.3 %copy-start = (s32[64]{0:T(128)}, s32[64]{0:T(128)S(1)}, u32[]{:S(2)}) copy-start(s32[64]{0:T(128)S(1)} %reshape.148.first) | copy-start | bytes 772
  19.2 70.1 %copy-start.1 = (s32[64]{0:T(128)}, s32[64]{0:T(128)S(1)}, u32[]{:S(2)}) copy-start(s32[64]{0:T(128)S(1)} %reshape.150.local) | copy-start | bytes 772
